TPU v7x, 32 devices: a whole 2x2x4 slice. The times are simulated.
32 devices in a mesh: grp: 2 (over x), col: 16 (over z, y, core).
Axes of the slice: x: 2, y: 2, z: 4, core: 2. Of those that a mesh axis runs over, the one named last changes fastest.
Arguments:
- mode_rows: float32 [16384, 256], P(('grp', 'col')), parts along dimension 0, may hold values from -8 to 8, as said below
- coeffs: bfloat16 [512, 256], P(('grp', 'col')), parts along dimension 0, may hold values from -18 to 18, as said below
- diffusivity: float32 [32, 64], P(('grp', 'col')), parts along dimension 0, may hold values from 0.02 to 0.24
- counts: int32 [32], P(('grp', 'col')), parts along dimension 0, may hold values from 32 to 64
- emis_idx: int32 [512], P('grp'), parts along dimension 0, may hold values from 0 to 15
- emis_table: float32 [16, 8], replicated, may hold values from 0.2 to 1.5
- reactants: int32 [12, 2], replicated, may hold values from 0 to 7
- stoich: int32 [12, 8], replicated, may hold values from -1 to 1
- rate_consts: float32 [12], replicated, may hold values from 0.02 to 0.2
- loss_rates: float32 [8], replicated, may hold values from 0.2 to 2
Outputs:
- modes_out: float32 [16384, 256], P(('grp', 'col')), parts along dimension 0
- coeffs_out: bfloat16 [512, 256], P(('grp', 'col')), parts along dimension 0
There are 2 independent parts, one for each index of `grp`. A program takes and returns all parts, laid end to end along the dimension named above; an argument that names none is the same for every part. Nothing has to cross between parts.
Inputs may be any that keep to these rules, and one draw needn't show every extreme that they name: `mode_rows`: modes of order one. `coeffs`: coefficients of order one.
All inputs are finite; a program needn't handle non-finite values.
Results may differ from a plain program's by a relative error of at most 0.0014.
The roundings to bfloat16 on the way count: a program that leaves them out, or rounds other values in their place, can miss the bound.
Values may be sent and summed in bfloat16 or wider, within the bound.
No kernel may reach another device: no remote copies, remote signals or barrier semaphores. Data moves between devices by JAX's collectives and lax.ppermute only.
A program may use at most 64 MiB of HBM per device.

v0:
```python
import math
import jax
import jax.numpy as jnp
from jax import lax
from jax.sharding import PartitionSpec as P

S = 8
LEV = 64
R = 256
NEMIS = 16
NSUB = 2
TIME_STEP = 0.1
RATE_STEP = 0.3
RIDGE_SHARE = 0.05
PRECISE = lax.Precision.HIGHEST


def diffuse(mode_block, diffusivity, counts):
    ncols = counts.shape[0]
    rank = mode_block.shape[1]
    blocked = mode_block.reshape(ncols, S, LEV, rank)
    level_index = jnp.arange(LEV, dtype=jnp.int32)
    face_coef = jnp.where(
        level_index[None, :] + 1 < counts[:, None], diffusivity, jnp.zeros_like(diffusivity)
    )
    upper_cells = jnp.concatenate([blocked[:, :, 1:], jnp.zeros_like(blocked[:, :, :1])], axis=2)
    face_flux = face_coef[:, None, :, None] * (upper_cells - blocked)
    lower_flux = jnp.concatenate(
        [jnp.zeros_like(face_flux[:, :, :1]), face_flux[:, :, :-1]], axis=2
    )
    return (blocked + face_flux - lower_flux).reshape(mode_block.shape)


def species_pick(table_column):
    return (table_column[:, None] == jnp.arange(S, dtype=jnp.int32)[None, :]).astype(jnp.float32)


def reaction(
    field_block,
    pick_first,
    pick_second,
    stoich_wide,
    rate_consts,
    loss_rates,
    emis_block,
    active,
    profile,
):
    first_amount = jnp.einsum("rs,bcsl->bcrl", pick_first, field_block, precision=PRECISE)
    second_amount = jnp.einsum("rs,bcsl->bcrl", pick_second, field_block, precision=PRECISE)
    reaction_speed = rate_consts[None, None, :, None] * first_amount * second_amount
    produced = jnp.einsum("rs,bcrl->bcsl", stoich_wide, reaction_speed, precision=PRECISE)
    tendency_raw = (
        produced
        - loss_rates[None, None, :, None] * field_block
        + emis_block[:, None, :, None] * profile[None, None, None, :]
    )
    return tendency_raw * active[None, :, None, :]


def on_device(
    mode_rows,
    coeffs,
    diffusivity,
    counts,
    emis_idx,
    emis_table,
    reactants,
    stoich,
    rate_consts,
    loss_rates,
):
    rows_dev = mode_rows.shape[0]
    mem_dev = coeffs.shape[0]
    col_count = lax.axis_size("col")
    total_rows = rows_dev * col_count
    members = mem_dev * col_count
    columns_dev = counts.shape[0]
    level_index = jnp.arange(LEV, dtype=jnp.int32)
    active = (level_index[None, :] < counts[:, None]).astype(jnp.float32)
    profile = jnp.exp(-4.0 * level_index.astype(jnp.float32) / LEV)
    chosen = (emis_idx[:, None] == jnp.arange(NEMIS, dtype=jnp.int32)[None, :]).astype(jnp.float32)
    member_emis = jnp.sum(chosen[:, :, None] * emis_table[None, :, :], axis=1)
    pick_first = species_pick(reactants[:, 0])
    pick_second = species_pick(reactants[:, 1])
    stoich_wide = stoich.astype(jnp.float32)
    rank_root = math.sqrt(R)
    inv_root = 1.0 / rank_root
    block_rows = math.gcd(members, 128)
    block_count = members // block_rows
    modes = mode_rows
    for substep in range(NSUB):
        diffused = diffuse(modes, diffusivity, counts)
        mode_bf = diffused.astype(jnp.bfloat16)
        rate_scale = rank_root / total_rows
        coef_gathered = lax.all_gather(coeffs, "col", axis=0, tiled=True)

        def member_block(pulled, block_inputs):
            coef_block, emis_block = block_inputs
            field_block = (
                lax.dot_general(
                    coef_block,
                    mode_bf,
                    (((1,), (1,)), ((), ())),
                    preferred_element_type=jnp.float32,
                )
                * inv_root
            )
            tendency = reaction(
                field_block.reshape(block_rows, columns_dev, S, LEV),
                pick_first,
                pick_second,
                stoich_wide,
                rate_consts,
                loss_rates,
                emis_block,
                active,
                profile,
            )
            tendency = tendency.reshape(block_rows, rows_dev).astype(jnp.bfloat16)
            pulled = pulled + lax.dot_general(
                tendency, coef_block, (((0,), (0,)), ((), ())), preferred_element_type=jnp.float32
            )
            part_rate = jnp.dot(tendency, mode_bf, preferred_element_type=jnp.float32)
            return (pulled, part_rate)

        pulled, rate_blocks = lax.scan(
            member_block,
            jnp.zeros((rows_dev, R), jnp.float32),
            (
                coef_gathered.reshape(block_count, block_rows, R),
                member_emis.reshape(block_count, block_rows, S),
            ),
        )
        pulled, rate_term = (pulled, rate_blocks.reshape(members, R))
        rate_mine = lax.psum_scatter(rate_term, "col", scatter_dimension=0, tiled=True) * rate_scale
        coef_wide = coeffs.astype(jnp.float32)
        gram_part = jnp.dot(coef_wide.T, coef_wide, precision=PRECISE)
        proj_part = lax.dot_general(
            mode_bf.astype(jnp.float32), pulled, (((0,), (0,)), ((), ())), precision=PRECISE
        )
        gram_matrix, proj_matrix = lax.psum((gram_part, proj_part), "col")
        proj_matrix = proj_matrix / total_rows
        gram_matrix = gram_matrix + RIDGE_SHARE * members * jnp.eye(R, dtype=jnp.float32)
        remainder = pulled - jnp.dot(diffused, proj_matrix, precision=PRECISE)
        factor = jnp.linalg.cholesky(gram_matrix)
        solved = jax.scipy.linalg.cho_solve((factor, True), remainder.T).T
        modes = diffused + TIME_STEP * rank_root * solved
        coeffs = (coef_wide + RATE_STEP * rate_mine).astype(jnp.bfloat16)
    return (modes, coeffs)


def solution(mesh):
    placed = (
        P(("grp", "col"), None),
        P(("grp", "col"), None),
        P(("grp", "col"), None),
        P(("grp", "col")),
        P("grp"),
        P(),
        P(),
        P(),
        P(),
        P(),
    )
    return jax.shard_map(
        on_device,
        mesh=mesh,
        in_specs=placed,
        out_specs=(P(("grp", "col"), None), P(("grp", "col"), None)),
        check_vma=False,
    )
```

profile of v0, /device:TPU:1, one launch (start us, length us, event | category | flops | bytes accessed | tf_op | source)
XLA Modules:
  0.0 393.6 jit_solution(5223242467514382098)
XLA Ops:
  7.2 23.6 %all_gather.6 = bf16[256,256]{1,0:T(8,128)(2,1)S(1)} all-gather(bf16[16,256]{1,0:T(8,128)(2,1)} %param.18), channel_id=1, replica_groups=mesh['grp'=2,'col'=16] {'col'}, dimensions={0}, use_global_device_ids=true | all-gather | bytes 139264 | tf_op jit(solution)/shard_map/all_gather | solution.py:96
  31.7 1.2 slice.80
  38.0 7.1 %while.30 = (s32[]{:T(128)}, f32[512,256]{1,0:T(8,128)S(1)}, f32[2,128,256]{2,1,0:T(8,128)S(1)}, f32[12]{0:T(128)S(1)}, bf16[2,128,256]{2,1,0:T(8,128)(2,1)S(1)}...) while((s32[]{:T(128)}, f32[512,256]{1,0:T(8,128)S(1)}, ...), condition=%wide.region_7.9_spmd.clone, body=%wide.region_6.8_spmd.clone.sunk | while | flops 129892992 | bytes 5650131 | solution.py:127
  45.1 1.2 fusion.103
  47.7 86.4 %all-reduce.12.cloned.1.call-done = (f32[256,256]{1,0:T(8,128)}, f32[256,256]{0,1:T(8,128)}) async-done(((f32[256,256]{1,0:T(8,128)}, f32[256,256]{0,1:T(8,128)}), (f32[256,256]{1,0:T(8,128)}, f32[256,256]{0,1:T(8,128)})) %all-reduce.12.cloned.1.call-update) | async-done | bytes 524304 | tf_op jit(solution)/shard_map/psum | solution.py:142
  136.1 11.7 %cholesky.130 = f32[128,128]{1,0:T(8,128)S(1)} custom-call(f32[128,128]{1,0:T(8,128)S(1)} %cholesky.194), custom_call_target="Cholesky" | custom-call | tf_op jit(solution)/shard_map/jit(cholesky)/cholesky | solution.py:146
  147.8 9.8 %custom-call.17 = f32[1,128,128]{1,2,0:T(8,128)S(1)} custom-call(f32[1,128,128]{2,1,0:T(8,128)S(1)} %get-tuple-element.369), custom_call_target="InvertDiagBlocksLowerTriangular" | custom-call | tf_op jit(solution)/shard_map/jit(cholesky)/cholesky | solution.py:146
  158.1 11.7 %cholesky.147 = f32[128,128]{1,0:T(8,128)S(1)} custom-call(f32[128,128]{1,0:T(8,128)S(1)} %convolution_subtract_fusion.7), custom_call_target="Cholesky" | custom-call | tf_op jit(solution)/shard_map/jit(cholesky)/cholesky | solution.py:146
  171.9 4.4 %while.32 = (s32[]{:T(128)}, f32[256,256]{1,0:T(8,128)S(1)}, s32[2,2]{1,0:T(2,128)S(1)}, f32[2,128,128]{2,1,0:T(8,128)S(1)}, s32[]{:T(128)}) while((s32[]{:T(128)}, f32[256,256]{1,0:T(8,128)S(1)}, s32[2,2]{1,0:T(2,128)S(1)}, f32[2,128,128]{2,1,0:T(8,128)S(1)}, s32[]{:T(128)}) %tuple.90), condition=%wide.while_cond, body=%wide.while_body.sunk | while | flops 2 | bytes 131181 | solution.py:147
  173.0 1.3 bitcast_dynamic-update-slice_fusion.4
  174.9 1.3 bitcast_dynamic-update-slice_fusion.4
  176.2 19.7 %custom-call.18 = f32[2,128,128]{1,2,0:T(8,128)S(1)} custom-call(f32[2,128,128]{2,1,0:T(8,128)S(1)} %get-tuple-element.258), custom_call_target="InvertDiagBlocksLowerTriangular" | custom-call | tf_op jit(solution)/shard_map/jit(_cho_solve)/triangular_solve | solution.py:147
  200.6 21.0 %all_gather.7 = bf16[256,256]{1,0:T(8,128)(2,1)S(1)} all-gather(bf16[16,256]{1,0:T(8,128)(2,1)S(1)} %add_convert_fusion.1), channel_id=1, replica_groups=mesh['grp'=2,'col'=16] {'col'}, dimensions={0}, use_global_device_ids=true | all-gather | bytes 139264 | tf_op jit(solution)/shard_map/all_gather | solution.py:96
  222.6 7.1 %while.31 = (s32[]{:T(128)}, f32[512,256]{1,0:T(8,128)S(1)}, f32[2,128,256]{2,1,0:T(8,128)S(1)}, f32[12]{0:T(128)S(1)}, bf16[2,128,256]{2,1,0:T(8,128)(2,1)S(1)}...) while((s32[]{:T(128)}, f32[512,256]{1,0:T(8,128)S(1)}, ...), condition=%wide.region_12.15_spmd.clone, body=%wide.region_11.14_spmd.clone.sunk | while | flops 129892992 | bytes 5650131 | solution.py:127
  229.7 1.2 fusion.105
  231.5 87.1 %all-reduce.10.cloned.1.call-done = (f32[256,256]{1,0:T(8,128)}, f32[256,256]{0,1:T(8,128)}) async-done(((f32[256,256]{1,0:T(8,128)}, f32[256,256]{0,1:T(8,128)}), (f32[256,256]{1,0:T(8,128)}, f32[256,256]{0,1:T(8,128)})) %all-reduce.10.cloned.1.call-update) | async-done | bytes 524304 | tf_op jit(solution)/shard_map/psum | solution.py:142
  320.6 11.7 %cholesky.164 = f32[128,128]{1,0:T(8,128)S(1)} custom-call(f32[128,128]{1,0:T(8,128)S(1)} %cholesky.197), custom_call_target="Cholesky" | custom-call | tf_op jit(solution)/shard_map/jit(cholesky)/cholesky | solution.py:146
  332.4 9.8 %custom-call.19 = f32[1,128,128]{1,2,0:T(8,128)S(1)} custom-call(f32[1,128,128]{2,1,0:T(8,128)S(1)} %get-tuple-element.365), custom_call_target="InvertDiagBlocksLowerTriangular" | custom-call | tf_op jit(solution)/shard_map/jit(cholesky)/cholesky | solution.py:146
  342.7 11.7 %cholesky.181 = f32[128,128]{1,0:T(8,128)S(1)} custom-call(f32[128,128]{1,0:T(8,128)S(1)} %convolution_subtract_fusion.6), custom_call_target="Cholesky" | custom-call | tf_op jit(solution)/shard_map/jit(cholesky)/cholesky | solution.py:146
  357.2 4.3 %while.33 = (s32[]{:T(128)}, f32[256,256]{1,0:T(8,128)S(1)}, s32[2,2]{1,0:T(2,128)S(1)}, f32[2,128,128]{2,1,0:T(8,128)S(1)}, s32[]{:T(128)}) while((s32[]{:T(128)}, f32[256,256]{1,0:T(8,128)S(1)}, s32[2,2]{1,0:T(2,128)S(1)}, f32[2,128,128]{2,1,0:T(8,128)S(1)}, s32[]{:T(128)}) %tuple.120), condition=%wide.while_cond.clone, body=%wide.while_body.clone.sunk | while | flops 2 | bytes 131181 | solution.py:147
  358.0 1.4 bitcast_dynamic-update-slice_fusion.5
  360.1 1.4 bitcast_dynamic-update-slice_fusion.5
  361.5 19.7 %custom-call.20 = f32[2,128,128]{1,2,0:T(8,128)S(1)} custom-call(f32[2,128,128]{2,1,0:T(8,128)S(1)} %get-tuple-element.259), custom_call_target="InvertDiagBlocksLowerTriangular" | custom-call | tf_op jit(solution)/shard_map/jit(_cho_solve)/triangular_solve | solution.py:147
  385.5 1.3 add_convert_fusion
  (159 shorter events, 40.4 us)
Async XLA Ops:
  7.2 126.9 %all-reduce.12.cloned.1.call-start = ((), (), s32[]{:S(2)}) async-start(), calls=%async_computation.5 | async-start | bytes 1048576 | tf_op jit(solution)/shard_map/psum | solution.py:142
  7.2 23.6 %copy-start.7 = (bf16[16,256]{1,0:T(8,128)(2,1)S(1)}, bf16[16,256]{1,0:T(8,128)(2,1)}, u32[]{:S(2)}) copy-start(bf16[16,256]{1,0:T(8,128)(2,1)} %param.18) | copy-start | bytes 24580
  31.7 2.5 copy-start
  33.6 0.7 copy-start.14
  34.5 0.7 copy-start.13
  35.2 0.7 copy-start.12
  35.9 0.7 copy-start.10
  36.6 0.7 copy-start.11
  37.4 0.7 copy-start.8
  37.4 0.7 copy-start.9
  45.1 1.2 copy-start.3
  46.3 153.5 %reduce-scatter.3.cloned.1.call-start = ((), (), s32[]{:S(2)}) async-start(), calls=%async_computation.2 | async-start | bytes 278528 | tf_op jit(solution)/shard_map/reduce_scatter | solution.py:136
  47.1 271.5 %all-reduce.10.cloned.1.call-start = ((), (), s32[]{:S(2)}) async-start(), calls=%async_computation.4 | async-start | bytes 1048576 | tf_op jit(solution)/shard_map/psum | solution.py:142
  135.1 1.0 copy-start.1
  171.9 24.1 %copy-start.5 = (f32[256,256]{1,0:T(8,128)S(1)}, f32[256,256]{1,0:T(8,128)}, u32[]{:S(2)}) copy-start(f32[256,256]{1,0:T(8,128)} %get-tuple-element.356) | copy-start | bytes 786436
  229.7 1.2 copy-start.4
  230.9 154.6 %reduce-scatter.5.cloned.1.call-start = ((), (), s32[]{:S(2)}) async-start(), calls=%async_computation.3 | async-start | bytes 278528 | tf_op jit(solution)/shard_map/reduce_scatter | solution.py:136
  319.6 1.0 copy-start.2
  357.2 24.0 %copy-start.6 = (f32[256,256]{1,0:T(8,128)S(1)}, f32[256,256]{1,0:T(8,128)}, u32[]{:S(2)}) copy-start(f32[256,256]{1,0:T(8,128)} %get-tuple-element.354) | copy-start | bytes 786436
Sparse Core Ops, SparseCore 0:
  46.5 87.5 all-reduce.11
  137.6 53.6 reduce-scatter.2
  231.0 87.5 all-reduce.9
  322.0 53.5 reduce-scatter.4
where the time goes:
time: 398 us; the launch traced here: 394 us
  waiting for transfers between devices  174 us (44%)
  other arithmetic  116 us (29%)
  blocking collectives  44.6 us (11%)
  matrix products  22 us (6%)
  between operations  17.7 us (4%)
  local copies, waits for them, and re-layouts  17.3 us (4%)
    psum x2, waiting for transfers between devices, on_device(): gram_matrix, proj_matrix = lax.psum((gram_part, proj_part), 'col')  174 us
    another operation x13, other arithmetic, on_device(): factor = jnp.linalg.cholesky(gram_matrix)  68.6 us
    all_gather x2, blocking collectives, on_device(): coef_gathered = lax.all_gather(coeffs, 'col', axis=0, tiled=True)  44.6 us
    another operation x5, other arithmetic, on_device(): solved = jax.scipy.linalg.cho_solve((factor, True), remainder.T).T  39.4 us
  transfers between devices with their start and end apart: 4, of which 2 were waited for; matrix products, arithmetic and copies ran while one was open for 32% of the time, Pallas kernels for 0%

commit v1 on v0

--- a/solution.py
+++ b/solution.py
@@ -93,7 +93,14 @@
         diffused = diffuse(modes, diffusivity, counts)
         mode_bf = diffused.astype(jnp.bfloat16)
         rate_scale = rank_root / total_rows
-        coef_gathered = lax.all_gather(coeffs, "col", axis=0, tiled=True)
+        ring = [coeffs]
+        for hop in range(15):
+            ring.append(lax.ppermute(ring[-1], "col", [(dev, (dev + 1) % 16) for dev in range(16)]))
+        coef_gathered = jnp.roll(
+            jnp.concatenate(ring[::-1], axis=0),
+            (lax.axis_index("col") + 1) * ring[0].shape[0],
+            axis=0,
+        )
 
         def member_block(pulled, block_inputs):
             coef_block, emis_block = block_inputs

time: 398 us -> 531 us (1.33)
  waiting for transfers between devices: 174 us -> 338 us
  blocking collectives: 44.6 us -> 0 us
  starting transfers between devices: 0.62 us -> 15.3 us
    ppermute x0 -> x30, waiting for transfers between devices: none -> 133 us  [on_device(): lax.ppermute(ring[-1], 'col', [(dev, (dev + 1) % 16) for dev in range(16)])]
    all_gather x2 -> x0, blocking collectives: 44.6 us -> none  [on_device(): coef_gathered = lax.all_gather(coeffs, 'col', axis=0, tiled=True)]
    reduce_scatter x2, waiting for transfers between devices: 0.02 us -> 21.2 us  [on_device(): lax.psum_scatter(rate_term, 'col', scatter_dimension=0, tiled=True)]
    ppermute x0 -> x30, starting transfers between devices: none -> 14.4 us  [on_device(): lax.ppermute(ring[-1], 'col', [(dev, (dev + 1) % 16) for dev in range(16)])]
    psum x2, waiting for transfers between devices: 174 us -> 184 us  [on_device(): gram_matrix, proj_matrix = lax.psum((gram_part, proj_part), 'col')]
  transfers between devices with their start and end apart: 4 -> 34, of which waited for: 2 -> 31; matrix products, arithmetic and copies ran while one was open for 32% -> 25% of each run, Pallas kernels for 0% -> 0%
where the time goes in v1:
time: 531 us; the launch traced here: 526 us
  waiting for transfers between devices  338 us (64%)
  other arithmetic  116 us (22%)
  matrix products  22 us (4%)
  between operations  18.1 us (3%)
  starting transfers between devices  15.3 us (3%)
  local copies, waits for them, and re-layouts  14.9 us (3%)
    psum x2, waiting for transfers between devices, on_device(): gram_matrix, proj_matrix = lax.psum((gram_part, proj_part), 'col')  184 us
    ppermute x30, waiting for transfers between devices, on_device(): lax.ppermute(ring[-1], 'col', [(dev, (dev + 1) % 16) for dev in range(16)])  133 us
    another operation x13, other arithmetic, on_device(): factor = jnp.linalg.cholesky(gram_matrix)  68.6 us
    another operation x5, other arithmetic, on_device(): solved = jax.scipy.linalg.cho_solve((factor, True), remainder.T).T  39.4 us
    reduce_scatter x2, waiting for transfers between devices, on_device(): lax.psum_scatter(rate_term, 'col', scatter_dimension=0, tiled=True)  21.2 us
    ppermute x30, starting transfers between devices, on_device(): lax.ppermute(ring[-1], 'col', [(dev, (dev + 1) % 16) for dev in range(16)])  14.4 us
  transfers between devices with their start and end apart: 34, of which 31 were waited for; matrix products, arithmetic and copies ran while one was open for 25% of the time, Pallas kernels for 0%

profile of v1, /device:TPU:1, one launch (start us, length us, event | category | flops | bytes accessed | tf_op | source)
XLA Modules:
  0.0 525.5 jit_solution(13208743976788440913)
XLA Ops:
  20.8 5.8 %collective-permute-done.3 = bf16[16,256]{1,0:T(8,128)(2,1)S(1)} collective-permute-done((bf16[16,256]{1,0:T(8,128)(2,1)S(1)}, bf16[16,256]{1,0:T(8,128)(2,1)S(1)}, u32[]{:S(2)}, u32[]{:S(2)}) %collective-permute-start.3) | collective-permute-done | bytes 8224 | tf_op jit(solution)/shard_map/ppermute | solution.py:98
  26.5 5.8 %collective-permute-done.4 = bf16[16,256]{1,0:T(8,128)(2,1)S(1)} collective-permute-done((bf16[16,256]{1,0:T(8,128)(2,1)S(1)}, bf16[16,256]{1,0:T(8,128)(2,1)S(1)}, u32[]{:S(2)}, u32[]{:S(2)}) %collective-permute-start.4) | collective-permute-done | bytes 8224 | tf_op jit(solution)/shard_map/ppermute | solution.py:98
  32.3 5.8 %collective-permute-done.5 = bf16[16,256]{1,0:T(8,128)(2,1)S(1)} collective-permute-done((bf16[16,256]{1,0:T(8,128)(2,1)S(1)}, bf16[16,256]{1,0:T(8,128)(2,1)S(1)}, u32[]{:S(2)}, u32[]{:S(2)}) %collective-permute-start.5) | collective-permute-done | bytes 8224 | tf_op jit(solution)/shard_map/ppermute | solution.py:98
  49.8 5.6 %collective-permute-done.8 = bf16[16,256]{1,0:T(8,128)(2,1)S(1)} collective-permute-done((bf16[16,256]{1,0:T(8,128)(2,1)S(1)}, bf16[16,256]{1,0:T(8,128)(2,1)S(1)}, u32[]{:S(2)}, u32[]{:S(2)}) %collective-permute-start.8) | collective-permute-done | bytes 8224 | tf_op jit(solution)/shard_map/ppermute | solution.py:98
  55.5 5.7 %collective-permute-done.9 = bf16[16,256]{1,0:T(8,128)(2,1)S(1)} collective-permute-done((bf16[16,256]{1,0:T(8,128)(2,1)S(1)}, bf16[16,256]{1,0:T(8,128)(2,1)S(1)}, u32[]{:S(2)}, u32[]{:S(2)}) %collective-permute-start.9) | collective-permute-done | bytes 8224 | tf_op jit(solution)/shard_map/ppermute | solution.py:98
  61.2 5.7 %collective-permute-done.10 = bf16[16,256]{1,0:T(8,128)(2,1)S(1)} collective-permute-done((bf16[16,256]{1,0:T(8,128)(2,1)S(1)}, bf16[16,256]{1,0:T(8,128)(2,1)S(1)}, u32[]{:S(2)}, u32[]{:S(2)}) %collective-permute-start.10) | collective-permute-done | bytes 8224 | tf_op jit(solution)/shard_map/ppermute | solution.py:98
  72.7 5.7 %collective-permute-done.12 = bf16[16,256]{1,0:T(8,128)(2,1)S(1)} collective-permute-done((bf16[16,256]{1,0:T(8,128)(2,1)S(1)}, bf16[16,256]{1,0:T(8,128)(2,1)S(1)}, u32[]{:S(2)}, u32[]{:S(2)}) %collective-permute-start.12) | collective-permute-done | bytes 8224 | tf_op jit(solution)/shard_map/ppermute | solution.py:98
  78.6 5.7 %collective-permute-done.13 = bf16[16,256]{1,0:T(8,128)(2,1)S(1)} collective-permute-done((bf16[16,256]{1,0:T(8,128)(2,1)S(1)}, bf16[16,256]{1,0:T(8,128)(2,1)S(1)}, u32[]{:S(2)}, u32[]{:S(2)}) %collective-permute-start.13) | collective-permute-done | bytes 8224 | tf_op jit(solution)/shard_map/ppermute | solution.py:98
  91.2 7.1 %while.30 = (s32[]{:T(128)}, f32[512,256]{1,0:T(8,128)S(1)}, f32[2,128,256]{2,1,0:T(8,128)S(1)}, f32[12]{0:T(128)S(1)}, bf16[2,128,256]{2,1,0:T(8,128)(2,1)S(1)}...) while((s32[]{:T(128)}, f32[512,256]{1,0:T(8,128)S(1)}, ...), condition=%wide.region_7.10_spmd.clone, body=%wide.region_6.9_spmd.clone.sunk | while | flops 129892992 | bytes 5650131 | solution.py:134
  100.8 91.8 %all-reduce.12.cloned.1.call-done = (f32[256,256]{1,0:T(8,128)}, f32[256,256]{0,1:T(8,128)}) async-done(((f32[256,256]{1,0:T(8,128)}, f32[256,256]{0,1:T(8,128)}), (f32[256,256]{1,0:T(8,128)}, f32[256,256]{0,1:T(8,128)})) %all-reduce.12.cloned.1.call-update) | async-done | bytes 524304 | tf_op jit(solution)/shard_map/psum | solution.py:149
  194.5 11.7 %cholesky.130 = f32[128,128]{1,0:T(8,128)S(1)} custom-call(f32[128,128]{1,0:T(8,128)S(1)} %cholesky.194), custom_call_target="Cholesky" | custom-call | tf_op jit(solution)/shard_map/jit(cholesky)/cholesky | solution.py:153
  206.3 9.8 %custom-call.17 = f32[1,128,128]{1,2,0:T(8,128)S(1)} custom-call(f32[1,128,128]{2,1,0:T(8,128)S(1)} %get-tuple-element.370), custom_call_target="InvertDiagBlocksLowerTriangular" | custom-call | tf_op jit(solution)/shard_map/jit(cholesky)/cholesky | solution.py:153
  216.6 11.7 %cholesky.147 = f32[128,128]{1,0:T(8,128)S(1)} custom-call(f32[128,128]{1,0:T(8,128)S(1)} %convolution_subtract_fusion.7), custom_call_target="Cholesky" | custom-call | tf_op jit(solution)/shard_map/jit(cholesky)/cholesky | solution.py:153
  228.4 21.2 %reduce-scatter.3.cloned.1.call-done = f32[16,256]{1,0:T(8,128)} async-done(((f32[256,256]{1,0:T(8,128)}), f32[16,256]{1,0:T(8,128)}) %reduce-scatter.3.cloned.1.call-update) | async-done | bytes 16400 | tf_op jit(solution)/shard_map/reduce_scatter | solution.py:143
  265.9 19.7 %custom-call.18 = f32[2,128,128]{1,2,0:T(8,128)S(1)} custom-call(f32[2,128,128]{2,1,0:T(8,128)S(1)} %get-tuple-element.259), custom_call_target="InvertDiagBlocksLowerTriangular" | custom-call | tf_op jit(solution)/shard_map/jit(_cho_solve)/triangular_solve | solution.py:154
  326.2 5.6 %collective-permute-done.26 = bf16[16,256]{1,0:T(8,128)(2,1)S(1)} collective-permute-done((bf16[16,256]{1,0:T(8,128)(2,1)S(1)}, bf16[16,256]{1,0:T(8,128)(2,1)S(1)}, u32[]{:S(2)}, u32[]{:S(2)}) %collective-permute-start.26) | collective-permute-done | bytes 8224 | tf_op jit(solution)/shard_map/ppermute | solution.py:98
  331.9 5.7 %collective-permute-done.27 = bf16[16,256]{1,0:T(8,128)(2,1)S(1)} collective-permute-done((bf16[16,256]{1,0:T(8,128)(2,1)S(1)}, bf16[16,256]{1,0:T(8,128)(2,1)S(1)}, u32[]{:S(2)}, u32[]{:S(2)}) %collective-permute-start.27) | collective-permute-done | bytes 8224 | tf_op jit(solution)/shard_map/ppermute | solution.py:98
  337.6 5.7 %collective-permute-done.28 = bf16[16,256]{1,0:T(8,128)(2,1)S(1)} collective-permute-done((bf16[16,256]{1,0:T(8,128)(2,1)S(1)}, bf16[16,256]{1,0:T(8,128)(2,1)S(1)}, u32[]{:S(2)}, u32[]{:S(2)}) %collective-permute-start.28) | collective-permute-done | bytes 8224 | tf_op jit(solution)/shard_map/ppermute | solution.py:98
  349.6 7.1 %while.31 = (s32[]{:T(128)}, f32[512,256]{1,0:T(8,128)S(1)}, f32[2,128,256]{2,1,0:T(8,128)S(1)}, f32[12]{0:T(128)S(1)}, bf16[2,128,256]{2,1,0:T(8,128)(2,1)S(1)}...) while((s32[]{:T(128)}, f32[512,256]{1,0:T(8,128)S(1)}, ...), condition=%wide.region_12.16_spmd.clone, body=%wide.region_11.15_spmd.clone.sunk | while | flops 129892992 | bytes 5650131 | solution.py:134
  358.5 92.0 %all-reduce.10.cloned.1.call-done = (f32[256,256]{1,0:T(8,128)}, f32[256,256]{0,1:T(8,128)}) async-done(((f32[256,256]{1,0:T(8,128)}, f32[256,256]{0,1:T(8,128)}), (f32[256,256]{1,0:T(8,128)}, f32[256,256]{0,1:T(8,128)})) %all-reduce.10.cloned.1.call-update) | async-done | bytes 524304 | tf_op jit(solution)/shard_map/psum | solution.py:149
  452.5 11.7 %cholesky.164 = f32[128,128]{1,0:T(8,128)S(1)} custom-call(f32[128,128]{1,0:T(8,128)S(1)} %cholesky.197), custom_call_target="Cholesky" | custom-call | tf_op jit(solution)/shard_map/jit(cholesky)/cholesky | solution.py:153
  464.3 9.8 %custom-call.19 = f32[1,128,128]{1,2,0:T(8,128)S(1)} custom-call(f32[1,128,128]{2,1,0:T(8,128)S(1)} %get-tuple-element.366), custom_call_target="InvertDiagBlocksLowerTriangular" | custom-call | tf_op jit(solution)/shard_map/jit(cholesky)/cholesky | solution.py:153
  474.6 11.7 %cholesky.181 = f32[128,128]{1,0:T(8,128)S(1)} custom-call(f32[128,128]{1,0:T(8,128)S(1)} %convolution_subtract_fusion.6), custom_call_target="Cholesky" | custom-call | tf_op jit(solution)/shard_map/jit(cholesky)/cholesky | solution.py:153
  493.4 19.7 %custom-call.20 = f32[2,128,128]{1,2,0:T(8,128)S(1)} custom-call(f32[2,128,128]{2,1,0:T(8,128)S(1)} %get-tuple-element.260), custom_call_target="InvertDiagBlocksLowerTriangular" | custom-call | tf_op jit(solution)/shard_map/jit(_cho_solve)/triangular_solve | solution.py:154
  (251 shorter events, 141.4 us)
Async XLA Ops:
  7.2 185.4 %all-reduce.12.cloned.1.call-start = ((), (), s32[]{:S(2)}) async-start(), calls=%async_computation.5 | async-start | bytes 1048576 | tf_op jit(solution)/shard_map/psum | solution.py:149
  15.0 5.8 %collective-permute-start.2 = (bf16[16,256]{1,0:T(8,128)(2,1)S(1)}, bf16[16,256]{1,0:T(8,128)(2,1)S(1)}, u32[]{:S(2)}, u32[]{:S(2)}) collective-permute-start(bf16[16,256]{1,0:T(8,128)(2,1)S(1)} %collective-permute-done.1), channel_id=1, source_target_pairs={{0,1},{1,2},{2,3},{3,4},{4,5},{5,6},{6,7},{7,8},{8,9},{9,10},{10,1... | collective-permute-start | bytes 24584 | tf_op jit(solution)/shard_map/ppermute | solution.py:98
  20.8 5.8 %collective-permute-start.3 = (bf16[16,256]{1,0:T(8,128)(2,1)S(1)}, bf16[16,256]{1,0:T(8,128)(2,1)S(1)}, u32[]{:S(2)}, u32[]{:S(2)}) collective-permute-start(bf16[16,256]{1,0:T(8,128)(2,1)S(1)} %collective-permute-done.2), channel_id=1, source_target_pairs={{0,1},{1,2},{2,3},{3,4},{4,5},{5,6},{6,7},{7,8},{8,9},{9,10},{10,1... | collective-permute-start | bytes 24584 | tf_op jit(solution)/shard_map/ppermute | solution.py:98
  26.5 5.8 %collective-permute-start.4 = (bf16[16,256]{1,0:T(8,128)(2,1)S(1)}, bf16[16,256]{1,0:T(8,128)(2,1)S(1)}, u32[]{:S(2)}, u32[]{:S(2)}) collective-permute-start(bf16[16,256]{1,0:T(8,128)(2,1)S(1)} %collective-permute-done.3), channel_id=1, source_target_pairs={{0,1},{1,2},{2,3},{3,4},{4,5},{5,6},{6,7},{7,8},{8,9},{9,10},{10,1... | collective-permute-start | bytes 24584 | tf_op jit(solution)/shard_map/ppermute | solution.py:98
  32.3 5.8 %collective-permute-start.5 = (bf16[16,256]{1,0:T(8,128)(2,1)S(1)}, bf16[16,256]{1,0:T(8,128)(2,1)S(1)}, u32[]{:S(2)}, u32[]{:S(2)}) collective-permute-start(bf16[16,256]{1,0:T(8,128)(2,1)S(1)} %collective-permute-done.4), channel_id=1, source_target_pairs={{0,1},{1,2},{2,3},{3,4},{4,5},{5,6},{6,7},{7,8},{8,9},{9,10},{10,1... | collective-permute-start | bytes 24584 | tf_op jit(solution)/shard_map/ppermute | solution.py:98
  38.1 5.8 %collective-permute-start.6 = (bf16[16,256]{1,0:T(8,128)(2,1)S(1)}, bf16[16,256]{1,0:T(8,128)(2,1)S(1)}, u32[]{:S(2)}, u32[]{:S(2)}) collective-permute-start(bf16[16,256]{1,0:T(8,128)(2,1)S(1)} %collective-permute-done.5), channel_id=1, source_target_pairs={{0,1},{1,2},{2,3},{3,4},{4,5},{5,6},{6,7},{7,8},{8,9},{9,10},{10,1... | collective-permute-start | bytes 24584 | tf_op jit(solution)/shard_map/ppermute | solution.py:98
  43.8 5.8 %collective-permute-start.7 = (bf16[16,256]{1,0:T(8,128)(2,1)S(1)}, bf16[16,256]{1,0:T(8,128)(2,1)S(1)}, u32[]{:S(2)}, u32[]{:S(2)}) collective-permute-start(bf16[16,256]{1,0:T(8,128)(2,1)S(1)} %collective-permute-done.6), channel_id=1, source_target_pairs={{0,1},{1,2},{2,3},{3,4},{4,5},{5,6},{6,7},{7,8},{8,9},{9,10},{10,1... | collective-permute-start | bytes 24584 | tf_op jit(solution)/shard_map/ppermute | solution.py:98
  49.6 5.8 %collective-permute-start.8 = (bf16[16,256]{1,0:T(8,128)(2,1)S(1)}, bf16[16,256]{1,0:T(8,128)(2,1)S(1)}, u32[]{:S(2)}, u32[]{:S(2)}) collective-permute-start(bf16[16,256]{1,0:T(8,128)(2,1)S(1)} %collective-permute-done.7), channel_id=1, source_target_pairs={{0,1},{1,2},{2,3},{3,4},{4,5},{5,6},{6,7},{7,8},{8,9},{9,10},{10,1... | collective-permute-start | bytes 24584 | tf_op jit(solution)/shard_map/ppermute | solution.py:98
  55.4 5.8 %collective-permute-start.9 = (bf16[16,256]{1,0:T(8,128)(2,1)S(1)}, bf16[16,256]{1,0:T(8,128)(2,1)S(1)}, u32[]{:S(2)}, u32[]{:S(2)}) collective-permute-start(bf16[16,256]{1,0:T(8,128)(2,1)S(1)} %collective-permute-done.8), channel_id=1, source_target_pairs={{0,1},{1,2},{2,3},{3,4},{4,5},{5,6},{6,7},{7,8},{8,9},{9,10},{10,1... | collective-permute-start | bytes 24584 | tf_op jit(solution)/shard_map/ppermute | solution.py:98
  61.2 5.8 %collective-permute-start.10 = (bf16[16,256]{1,0:T(8,128)(2,1)S(1)}, bf16[16,256]{1,0:T(8,128)(2,1)S(1)}, u32[]{:S(2)}, u32[]{:S(2)}) collective-permute-start(bf16[16,256]{1,0:T(8,128)(2,1)S(1)} %collective-permute-done.9), channel_id=1, source_target_pairs={{0,1},{1,2},{2,3},{3,4},{4,5},{5,6},{6,7},{7,8},{8,9},{9,10},{10,1... | collective-permute-start | bytes 24584 | tf_op jit(solution)/shard_map/ppermute | solution.py:98
  66.9 5.8 %collective-permute-start.11 = (bf16[16,256]{1,0:T(8,128)(2,1)S(1)}, bf16[16,256]{1,0:T(8,128)(2,1)S(1)}, u32[]{:S(2)}, u32[]{:S(2)}) collective-permute-start(bf16[16,256]{1,0:T(8,128)(2,1)S(1)} %collective-permute-done.10), channel_id=1, source_target_pairs={{0,1},{1,2},{2,3},{3,4},{4,5},{5,6},{6,7},{7,8},{8,9},{9,10},{10,1... | collective-permute-start | bytes 24584 | tf_op jit(solution)/shard_map/ppermute | solution.py:98
  72.7 5.8 %collective-permute-start.12 = (bf16[16,256]{1,0:T(8,128)(2,1)S(1)}, bf16[16,256]{1,0:T(8,128)(2,1)S(1)}, u32[]{:S(2)}, u32[]{:S(2)}) collective-permute-start(bf16[16,256]{1,0:T(8,128)(2,1)S(1)} %collective-permute-done.11), channel_id=1, source_target_pairs={{0,1},{1,2},{2,3},{3,4},{4,5},{5,6},{6,7},{7,8},{8,9},{9,10},{10,1... | collective-permute-start | bytes 24584 | tf_op jit(solution)/shard_map/ppermute | solution.py:98
  78.5 5.8 %collective-permute-start.13 = (bf16[16,256]{1,0:T(8,128)(2,1)S(1)}, bf16[16,256]{1,0:T(8,128)(2,1)S(1)}, u32[]{:S(2)}, u32[]{:S(2)}) collective-permute-start(bf16[16,256]{1,0:T(8,128)(2,1)S(1)} %collective-permute-done.12), channel_id=1, source_target_pairs={{0,1},{1,2},{2,3},{3,4},{4,5},{5,6},{6,7},{7,8},{8,9},{9,10},{10,1... | collective-permute-start | bytes 24584 | tf_op jit(solution)/shard_map/ppermute | solution.py:98
  84.3 5.8 %collective-permute-start.14 = (bf16[16,256]{1,0:T(8,128)(2,1)S(1)}, bf16[16,256]{1,0:T(8,128)(2,1)S(1)}, u32[]{:S(2)}, u32[]{:S(2)}) collective-permute-start(bf16[16,256]{1,0:T(8,128)(2,1)S(1)} %collective-permute-done.13), channel_id=1, source_target_pairs={{0,1},{1,2},{2,3},{3,4},{4,5},{5,6},{6,7},{7,8},{8,9},{9,10},{10,1... | collective-permute-start | bytes 24584 | tf_op jit(solution)/shard_map/ppermute | solution.py:98
  99.5 150.1 %reduce-scatter.3.cloned.1.call-start = ((), (), s32[]{:S(2)}) async-start(), calls=%async_computation.2 | async-start | bytes 278528 | tf_op jit(solution)/shard_map/reduce_scatter | solution.py:143
  100.2 350.3 %all-reduce.10.cloned.1.call-start = ((), (), s32[]{:S(2)}) async-start(), calls=%async_computation.4 | async-start | bytes 1048576 | tf_op jit(solution)/shard_map/psum | solution.py:149
  259.3 5.8 %collective-permute-start.17 = (bf16[16,256]{1,0:T(8,128)(2,1)S(1)}, bf16[16,256]{1,0:T(8,128)(2,1)S(1)}, u32[]{:S(2)}, u32[]{:S(2)}) collective-permute-start(bf16[16,256]{1,0:T(8,128)(2,1)S(1)} %collective-permute-done.16), channel_id=1, source_target_pairs={{0,1},{1,2},{2,3},{3,4},{4,5},{5,6},{6,7},{7,8},{8,9},{9,10},{10,1... | collective-permute-start | bytes 24584 | tf_op jit(solution)/shard_map/ppermute | solution.py:98
  265.1 20.5 %collective-permute-start.18 = (bf16[16,256]{1,0:T(8,128)(2,1)S(1)}, bf16[16,256]{1,0:T(8,128)(2,1)S(1)}, u32[]{:S(2)}, u32[]{:S(2)}) collective-permute-start(bf16[16,256]{1,0:T(8,128)(2,1)S(1)} %collective-permute-done.17), channel_id=1, source_target_pairs={{0,1},{1,2},{2,3},{3,4},{4,5},{5,6},{6,7},{7,8},{8,9},{9,10},{10,1... | collective-permute-start | bytes 24584 | tf_op jit(solution)/shard_map/ppermute | solution.py:98
  285.6 5.8 %collective-permute-start.19 = (bf16[16,256]{1,0:T(8,128)(2,1)S(1)}, bf16[16,256]{1,0:T(8,128)(2,1)S(1)}, u32[]{:S(2)}, u32[]{:S(2)}) collective-permute-start(bf16[16,256]{1,0:T(8,128)(2,1)S(1)} %collective-permute-done.18), channel_id=1, source_target_pairs={{0,1},{1,2},{2,3},{3,4},{4,5},{5,6},{6,7},{7,8},{8,9},{9,10},{10,1... | collective-permute-start | bytes 24584 | tf_op jit(solution)/shard_map/ppermute | solution.py:98
  297.2 5.8 %collective-permute-start.21 = (bf16[16,256]{1,0:T(8,128)(2,1)S(1)}, bf16[16,256]{1,0:T(8,128)(2,1)S(1)}, u32[]{:S(2)}, u32[]{:S(2)}) collective-permute-start(bf16[16,256]{1,0:T(8,128)(2,1)S(1)} %collective-permute-done.20), channel_id=1, source_target_pairs={{0,1},{1,2},{2,3},{3,4},{4,5},{5,6},{6,7},{7,8},{8,9},{9,10},{10,1... | collective-permute-start | bytes 24584 | tf_op jit(solution)/shard_map/ppermute | solution.py:98
  302.9 5.8 %collective-permute-start.22 = (bf16[16,256]{1,0:T(8,128)(2,1)S(1)}, bf16[16,256]{1,0:T(8,128)(2,1)S(1)}, u32[]{:S(2)}, u32[]{:S(2)}) collective-permute-start(bf16[16,256]{1,0:T(8,128)(2,1)S(1)} %collective-permute-done.21), channel_id=1, source_target_pairs={{0,1},{1,2},{2,3},{3,4},{4,5},{5,6},{6,7},{7,8},{8,9},{9,10},{10,1... | collective-permute-start | bytes 24584 | tf_op jit(solution)/shard_map/ppermute | solution.py:98
  308.7 5.8 %collective-permute-start.23 = (bf16[16,256]{1,0:T(8,128)(2,1)S(1)}, bf16[16,256]{1,0:T(8,128)(2,1)S(1)}, u32[]{:S(2)}, u32[]{:S(2)}) collective-permute-start(bf16[16,256]{1,0:T(8,128)(2,1)S(1)} %collective-permute-done.22), channel_id=1, source_target_pairs={{0,1},{1,2},{2,3},{3,4},{4,5},{5,6},{6,7},{7,8},{8,9},{9,10},{10,1... | collective-permute-start | bytes 24584 | tf_op jit(solution)/shard_map/ppermute | solution.py:98
  314.5 5.8 %collective-permute-start.24 = (bf16[16,256]{1,0:T(8,128)(2,1)S(1)}, bf16[16,256]{1,0:T(8,128)(2,1)S(1)}, u32[]{:S(2)}, u32[]{:S(2)}) collective-permute-start(bf16[16,256]{1,0:T(8,128)(2,1)S(1)} %collective-permute-done.23), channel_id=1, source_target_pairs={{0,1},{1,2},{2,3},{3,4},{4,5},{5,6},{6,7},{7,8},{8,9},{9,10},{10,1... | collective-permute-start | bytes 24584 | tf_op jit(solution)/shard_map/ppermute | solution.py:98
  357.9 159.5 %reduce-scatter.5.cloned.1.call-start = ((), (), s32[]{:S(2)}) async-start(), calls=%async_computation.3 | async-start | bytes 278528 | tf_op jit(solution)/shard_map/reduce_scatter | solution.py:143
  (25 other events, 131.5 us)
Sparse Core Ops, SparseCore 0:
  99.6 92.9 all-reduce.11
  196.1 53.4 reduce-scatter.2
  358.0 92.4 all-reduce.9
  453.9 53.6 reduce-scatter.4
